TPU v7x, 128 devices: a whole 4x4x4 slice. The times are simulated.
128 devices in a mesh: exp: 8 (over x, core), fsdp: 16 (over z, y).
Axes of the slice: x: 4, y: 4, z: 4, core: 2. Of those that a mesh axis runs over, the one named last changes fastest.
Arguments:
- tokens: bfloat16 [16384, 1536], P(('exp', 'fsdp')), may hold values from -6 to 6
- expert_ids: int32 [16384, 2], P(('exp', 'fsdp')), may hold values from 0 to 7, all different within a row; in each aligned block of 128 rows (0 to 127, 128 to 255, ...) at most 48 rows name the same one
- gates: float32 [16384, 2], P(('exp', 'fsdp')), may hold values from 0.1 to 1
- w_in: bfloat16 [8, 2048, 1536], P('exp', 'fsdp'), may hold values from -0.15625 to 0.15625
- w_out: bfloat16 [8, 2048, 1536], P('exp', 'fsdp'), may hold values from -0.125 to 0.125
- grad_y: bfloat16 [16384, 1536], P(('exp', 'fsdp')), may hold values from -6 to 6
Outputs:
- mixed: bfloat16 [16384, 1536], P(('exp', 'fsdp'))
- grad_tokens: bfloat16 [16384, 1536], P(('exp', 'fsdp'))
- grad_w_in: float32 [8, 2048, 1536], P('exp', 'fsdp')
- grad_w_out: float32 [8, 2048, 1536], P('exp', 'fsdp')
- grad_gates: float32 [16384, 2], P(('exp', 'fsdp'))
Inputs may be any that keep to these rules, and one draw needn't show every extreme that they name: `expert_ids`: each row names two different experts. Among the rows of one device no expert is named by more than 48 rows, and in some device some expert is named by exactly 48 rows.
All inputs are finite; a program needn't handle non-finite values.
Results may differ from a plain program's by a relative error of at most 0.0065.
Values may be sent and summed in bfloat16 or wider, within the bound.
A program may use at most 192 MiB of HBM per device.

v0:
```python
import jax
import jax.numpy as jnp
from jax import lax
from jax.sharding import PartitionSpec as P

inv_sqrt_two = 0.7071067811865476
inv_sqrt_two_pi = 0.3989422804014327


def gelu_parts(values):
    cdf_part = 0.5 * (1.0 + jax.scipy.special.erf(values * inv_sqrt_two))
    return (
        values * cdf_part,
        cdf_part + values * jnp.exp(-0.5 * values * values) * inv_sqrt_two_pi,
    )


def contract_first(left, right):
    return lax.dot_general(
        left, right, (((0,), (0,)), ((), ())), preferred_element_type=jnp.float32
    )


def contract_last(left, right):
    return lax.dot_general(
        left, right, (((1,), (1,)), ((), ())), preferred_element_type=jnp.float32
    )


def shards(tokens, expert_ids, gates, w_in, w_out, grad_y):
    tok_rows, features = tokens.shape
    groups = lax.axis_size("exp")
    capacity = 3 * tok_rows // groups
    slot_count = 2 * tok_rows
    buffer_rows = groups * capacity
    flat_ids = expert_ids.reshape(-1)
    onehot = (flat_ids[:, None] == jnp.arange(groups, dtype=jnp.int32)[None, :]).astype(jnp.int32)
    slot_rank = jnp.sum((jnp.cumsum(onehot, axis=0) - 1) * onehot, axis=1)
    slot_index = flat_ids * capacity + slot_rank
    token_slots = jnp.repeat(tokens, 2, axis=0)
    grad_slots = (
        (gates[:, :, None] * grad_y[:, None, :]).astype(jnp.bfloat16).reshape(slot_count, features)
    )
    send_tokens = jnp.zeros((buffer_rows, features), jnp.bfloat16).at[slot_index].set(token_slots)
    send_grads = jnp.zeros((buffer_rows, features), jnp.bfloat16).at[slot_index].set(grad_slots)
    recv_tokens, recv_grads = (
        lax.all_to_all(
            send_tokens.reshape(groups, capacity, features),
            "exp",
            split_axis=0,
            concat_axis=0,
            tiled=True,
        ),
        lax.all_to_all(
            send_grads.reshape(groups, capacity, features),
            "exp",
            split_axis=0,
            concat_axis=0,
            tiled=True,
        ),
    )
    recv_tokens = recv_tokens.reshape(buffer_rows, features)
    recv_grads = recv_grads.reshape(buffer_rows, features)
    full_in, full_out = (
        lax.all_gather(w_in, "fsdp", axis=1, tiled=True),
        lax.all_gather(w_out, "fsdp", axis=1, tiled=True),
    )
    full_in = full_in[0]
    full_out = full_out[0]
    hidden_pre = contract_last(recv_tokens, full_in)
    act_full, slope_term = gelu_parts(hidden_pre)
    act_bf = act_full.astype(jnp.bfloat16)
    expert_out = jnp.dot(act_bf, full_out, preferred_element_type=jnp.float32).astype(jnp.bfloat16)
    expert_out = expert_out.reshape(groups, capacity, features)
    back_out = lax.all_to_all(expert_out, "exp", split_axis=0, concat_axis=0, tiled=True)
    again_in, again_out = (
        lax.all_gather(w_in, "fsdp", axis=1, tiled=True),
        lax.all_gather(w_out, "fsdp", axis=1, tiled=True),
    )
    back_in_weight = again_in[0]
    back_out_weight = again_out[0]
    grad_act = contract_last(recv_grads, back_out_weight)
    grad_hidden = (grad_act * slope_term).astype(jnp.bfloat16)
    input_grad = jnp.dot(grad_hidden, back_in_weight, preferred_element_type=jnp.float32).astype(
        jnp.bfloat16
    )
    input_grad = input_grad.reshape(groups, capacity, features)
    back_input = lax.all_to_all(input_grad, "exp", split_axis=0, concat_axis=0, tiled=True)
    out_three = (
        back_out.reshape(buffer_rows, features)[slot_index]
        .reshape(tok_rows, 2, features)
        .astype(jnp.float32)
    )
    mixed = jnp.sum(gates[:, :, None] * out_three, axis=1).astype(jnp.bfloat16)
    grad_gates = jnp.sum(grad_y.astype(jnp.float32)[:, None, :] * out_three, axis=-1)
    input_three = (
        back_input.reshape(buffer_rows, features)[slot_index]
        .reshape(tok_rows, 2, features)
        .astype(jnp.float32)
    )
    grad_tokens = jnp.sum(input_three, axis=1).astype(jnp.bfloat16)
    summed = lax.psum_scatter(
        jnp.concatenate(
            [contract_first(grad_hidden, recv_tokens), contract_first(act_bf, recv_grads)], axis=1
        ),
        "fsdp",
        scatter_dimension=0,
        tiled=True,
    )
    grad_in = summed[:, :features]
    grad_out = summed[:, features:]
    return (mixed, grad_tokens, grad_in[None], grad_out[None], grad_gates)


def solution(mesh):
    return jax.shard_map(
        shards,
        mesh=mesh,
        in_specs=(
            P(("exp", "fsdp"), None),
            P(("exp", "fsdp"), None),
            P(("exp", "fsdp"), None),
            P("exp", "fsdp", None),
            P("exp", "fsdp", None),
            P(("exp", "fsdp"), None),
        ),
        out_specs=(
            P(("exp", "fsdp"), None),
            P(("exp", "fsdp"), None),
            P("exp", "fsdp", None),
            P("exp", "fsdp", None),
            P(("exp", "fsdp"), None),
        ),
        check_vma=False,
    )
```

profile of v0, /device:TPU:1, one launch (start us, length us, event | category | flops | bytes accessed | tf_op | source)
XLA Modules:
  0.0 329.9 jit_solution(15037019485016087798)
XLA Ops:
  7.2 0.7 all-gather.3.cloned.1.call-update
  7.9 0.7 all-gather.5.cloned.1.call-update
  8.6 0.8 copy.23
  9.4 0.1 eq.29
  9.6 0.1 eq.25
  9.7 0.7 broadcast_multiply_fusion
  10.4 0.1 copy.22
  10.5 0.1 mul.94
  10.7 0.6 reduce-window.6
  11.3 0.2 slice_reduce_fusion
  11.5 1.4 broadcast_in_dim.6
  12.9 0.3 reshape.140
  13.2 0.1 fusion.27
  13.4 2.9 scatter_custom_fusion
  16.3 5.8 %all-to-all-start = ((bf16[8,48,1536]{2,1,0:T(8,128)(2,1)}), bf16[8,48,1536]{2,1,0:T(8,128)(2,1)}, u32[]{:S(2)}, u32[]{:S(2)}) async-start(bf16[8,48,1536]{2,1,0:T(8,128)(2,1)} %bitcast.4), calls=%async_computation | async-start | bytes 2359296 | tf_op jit(solution)/shard_map/all_to_all | solution.py:47
  22.1 0.1 copy.21
  22.2 0.1 mul.102
  22.3 0.5 copy-done.3
  22.8 0.4 mul.104
  23.2 1.1 mul.105
  24.3 3.0 scatter_custom_fusion.1
  27.3 11.2 %all-to-all-done = bf16[8,48,1536]{2,1,0:T(8,128)(2,1)} async-done(((bf16[8,48,1536]{2,1,0:T(8,128)(2,1)}), bf16[8,48,1536]{2,1,0:T(8,128)(2,1)}, u32[]{:S(2)}, u32[]{:S(2)}) %all-to-all-start) | async-done | bytes 1179680 | tf_op jit(solution)/shard_map/all_to_all | solution.py:47
  38.5 4.4 %all-to-all-start.2 = ((bf16[8,48,1536]{2,1,0:T(8,128)(2,1)}), bf16[8,48,1536]{2,1,0:T(8,128)(2,1)S(1)}, u32[]{:S(2)}, u32[]{:S(2)}) async-start(bf16[8,48,1536]{2,1,0:T(8,128)(2,1)} %bitcast.10), calls=%async_computation.2 | async-start | bytes 2359296 | tf_op jit(solution)/shard_map/all_to_all | solution.py:54
  43.0 31.6 %all-gather.3.cloned.1.call-done = bf16[1,2048,1536]{2,1,0:T(8,128)(2,1)} async-done(((bf16[1,128,1536]{2,1,0:T(8,128)(2,1)}), bf16[1,2048,1536]{2,1,0:T(8,128)(2,1)}) %all-gather.3.cloned.1.call-update) | async-done | bytes 6291472 | tf_op jit(solution)/shard_map/all_gather | solution.py:65
  74.6 7.5 %multiply_convert_fusion = (bf16[384,2048]{1,0:T(8,128)(2,1)S(1)}, f32[384,2048]{1,0:T(8,128)}) fusion(bf16[384,1536]{1,0:T(8,128)(2,1)} %bitcast.5, bf16[1,2048,1536]{2,1,0:T(8,128)(2,1)} %all-gather.3.cloned.1.call-done), kind=kOutput, calls=%fused_computation.20 | convolution fusion | flops 2419851264 | bytes 12189696 | tf_op jit(solution)/shard_map/dot_general | solution.py:25
  82.1 55.6 %all-gather.5.cloned.1.call-done = bf16[1,2048,1536]{2,1,0:T(8,128)(2,1)} async-done(((bf16[1,128,1536]{2,1,0:T(8,128)(2,1)}), bf16[1,2048,1536]{2,1,0:T(8,128)(2,1)}) %all-gather.5.cloned.1.call-update) | async-done | bytes 6291472 | tf_op jit(solution)/shard_map/all_gather | solution.py:66
  137.7 7.8 %fusion.13 = bf16[384,2048]{1,0:T(8,128)(2,1)S(1)} fusion(f32[384,2048]{1,0:T(8,128)} %get-tuple-element.25, bf16[384,1536]{1,0:T(8,128)(2,1)S(1)} %bitcast.50, bf16[1,2048,1536]{2,1,0:T(8,128)(2,1)} %all-gather.5.cloned.1.call-done), kind=kOutput, calls=%fused_computation.19 | convolution fusion | flops 2423783424 | bytes 12189696 | tf_op jit(solution)/shard_map/dot_general | solution.py:25
  145.5 5.3 %fusion.29 = f32[2048,1536]{0,1:T(8,128)S(1)} fusion(bf16[384,2048]{1,0:T(8,128)(2,1)S(1)} %fusion.13, bf16[384,1536]{1,0:T(8,128)(2,1)} %bitcast.5), kind=kOutput, calls=%fused_computation.43 | convolution fusion | flops 2415919104 | bytes 15335424 | tf_op jit(solution)/shard_map/dot_general | solution.py:19
  150.9 3.5 %fusion.30 = f32[2048,1536]{0,1:T(8,128)S(1)} fusion(bf16[384,2048]{1,0:T(8,128)(2,1)S(1)} %get-tuple-element.24, bf16[384,1536]{1,0:T(8,128)(2,1)S(1)} %bitcast.51), kind=kOutput, calls=%fused_computation.44 | convolution fusion | flops 2415919104 | bytes 15335424 | tf_op jit(solution)/shard_map/dot_general | solution.py:19
  154.3 12.1 %pad_maximum_fusion = f32[2048,3072]{0,1:T(8,128)} fusion(f32[2048,1536]{0,1:T(8,128)S(1)} %fusion.30, f32[2048,1536]{0,1:T(8,128)S(1)} %fusion.29), kind=kLoop, calls=%fused_computation.4 | loop fusion | flops 6291456 | bytes 50331648 | tf_op jit(solution)/shard_map/concatenate | solution.py:103
  166.5 6.4 %fusion.19 = bf16[384,1536]{1,0:T(8,128)(2,1)} fusion(bf16[384,2048]{1,0:T(8,128)(2,1)S(1)} %get-tuple-element.24, bf16[1,2048,1536]{2,1,0:T(8,128)(2,1)} %all-gather.5.cloned.1.call-done), kind=kOutput, calls=%fused_computation.23 | convolution fusion | flops 2416508928 | bytes 9043968 | tf_op jit(solution)/shard_map/dot_general | solution.py:73
  172.9 5.2 %all-to-all-start.1 = ((bf16[8,48,1536]{2,1,0:T(8,128)(2,1)}), bf16[8,48,1536]{2,1,0:T(8,128)(2,1)S(1)}, u32[]{:S(2)}, u32[]{:S(2)}) async-start(bf16[8,48,1536]{2,1,0:T(8,128)(2,1)} %bitcast.53), calls=%async_computation.1 | async-start | bytes 2359296 | tf_op jit(solution)/shard_map/all_to_all | solution.py:75
  178.1 6.4 %fusion.16 = bf16[384,1536]{1,0:T(8,128)(2,1)} fusion(bf16[384,2048]{1,0:T(8,128)(2,1)S(1)} %copy-done.1, bf16[1,2048,1536]{2,1,0:T(8,128)(2,1)} %all-gather.3.cloned.1.call-done), kind=kOutput, calls=%fused_computation.22 | convolution fusion | flops 2416508928 | bytes 9043968 | tf_op jit(solution)/shard_map/dot_general | solution.py:84
  184.5 10.0 %all-to-all-done.1 = bf16[8,48,1536]{2,1,0:T(8,128)(2,1)S(1)} async-done(((bf16[8,48,1536]{2,1,0:T(8,128)(2,1)}), bf16[8,48,1536]{2,1,0:T(8,128)(2,1)S(1)}, u32[]{:S(2)}, u32[]{:S(2)}) %all-to-all-start.1) | async-done | bytes 1179680 | tf_op jit(solution)/shard_map/all_to_all | solution.py:75
  194.5 4.4 %all-to-all-start.3 = ((bf16[8,48,1536]{2,1,0:T(8,128)(2,1)}), bf16[8,48,1536]{2,1,0:T(8,128)(2,1)S(1)}, u32[]{:S(2)}, u32[]{:S(2)}) async-start(bf16[8,48,1536]{2,1,0:T(8,128)(2,1)} %bitcast.52), calls=%async_computation.3 | async-start | bytes 2359296 | tf_op jit(solution)/shard_map/all_to_all | solution.py:88
  198.9 0.1 convert_element_type.47
  199.0 2.1 gather_fusion
  201.2 14.2 %all-to-all-done.3 = bf16[8,48,1536]{2,1,0:T(8,128)(2,1)S(1)} async-done(((bf16[8,48,1536]{2,1,0:T(8,128)(2,1)}), bf16[8,48,1536]{2,1,0:T(8,128)(2,1)S(1)}, u32[]{:S(2)}, u32[]{:S(2)}) %all-to-all-start.3) | async-done | bytes 1179680 | tf_op jit(solution)/shard_map/all_to_all | solution.py:88
  215.3 2.1 gather_fusion.1
  217.5 2.2 reshape.118
  219.7 2.9 reduce_sum.44
  222.5 2.2 reshape.119
  224.7 3.5 %multiply_reduce_fusion = (f32[128,2]{1,0:T(8,128)S(1)}, bf16[128,1536]{1,0:T(8,128)(2,1)}) fusion(f32[128,2,1536]{2,1,0:T(2,128)S(1)} %reshape.119, f32[128,1536]{1,0:T(8,128)S(1)} %convert_element_type.47, f32[128,2]{1,0:T(8,128)S(1)} %copy-done.4), kind=kLoop, calls=%fused_computation.24 | loop fusion | flops 1376000 | bytes 2754560 | tf_op jit(solution)/shard_map/reduce_sum | solution.py:95
  228.3 0.6 copy.28
  228.9 90.7 %reduce-scatter.2.cloned.1.call-done = f32[128,3072]{0,1:T(8,128)} async-done(((f32[2048,3072]{0,1:T(8,128)}), f32[128,3072]{0,1:T(8,128)}) %reduce-scatter.2.cloned.1.call-update) | async-done | bytes 1572880 | tf_op jit(solution)/shard_map/reduce_scatter | solution.py:102
  319.6 1.5 slice_bitcast_fusion
  321.0 1.1 copy.27
  322.2 1.1 copy.26
  (21 shorter events, 0.2 us)
Async XLA Ops:
  7.2 67.4 %all-gather.3.cloned.1.call-start = ((), (), s32[]{:S(2)}) async-start(), calls=%async_computation.5 | async-start | bytes 6684672 | tf_op jit(solution)/shard_map/all_gather | solution.py:65
  7.9 129.8 %all-gather.5.cloned.1.call-start = ((), (), s32[]{:S(2)}) async-start(), calls=%async_computation.6 | async-start | bytes 6684672 | tf_op jit(solution)/shard_map/all_gather | solution.py:66
  13.3 8.7 %copy-start.5 = (f32[128,2]{0,1:T(2,128)S(1)}, f32[128,2]{0,1:T(2,128)}, u32[]{:S(2)}) copy-start(f32[128,2]{0,1:T(2,128)} %param.8) | copy-start | bytes 3076
  13.3 9.5 %copy-start.2 = (bf16[128,1536]{1,0:T(8,128)(2,1)S(1)}, bf16[128,1536]{1,0:T(8,128)(2,1)}, u32[]{:S(2)}) copy-start(bf16[128,1536]{1,0:T(8,128)(2,1)} %param.11) | copy-start | bytes 1179652
  16.3 22.3 %all-to-all-start = ((bf16[8,48,1536]{2,1,0:T(8,128)(2,1)}), bf16[8,48,1536]{2,1,0:T(8,128)(2,1)}, u32[]{:S(2)}, u32[]{:S(2)}) async-start(bf16[8,48,1536]{2,1,0:T(8,128)(2,1)} %bitcast.4), calls=%async_computation | async-start | bytes 2359296 | tf_op jit(solution)/shard_map/all_to_all | solution.py:47
  22.2 0.6 copy-start.3
  38.5 43.5 %all-to-all-start.2 = ((bf16[8,48,1536]{2,1,0:T(8,128)(2,1)}), bf16[8,48,1536]{2,1,0:T(8,128)(2,1)S(1)}, u32[]{:S(2)}, u32[]{:S(2)}) async-start(bf16[8,48,1536]{2,1,0:T(8,128)(2,1)} %bitcast.10), calls=%async_computation.2 | async-start | bytes 2359296 | tf_op jit(solution)/shard_map/all_to_all | solution.py:54
  43.0 276.6 %reduce-scatter.2.cloned.1.call-start = ((), (), s32[]{:S(2)}) async-start(), calls=%async_computation.7 | async-start | bytes 26738688 | tf_op jit(solution)/shard_map/reduce_scatter | solution.py:102
  145.5 5.3 %copy-start = (bf16[384,2048]{1,0:T(8,128)(2,1)}, bf16[384,2048]{1,0:T(8,128)(2,1)S(1)}, u32[]{:S(2)}) copy-start(bf16[384,2048]{1,0:T(8,128)(2,1)S(1)} %fusion.13) | copy-start | bytes 4718596
  172.9 5.2 %copy-start.1 = (bf16[384,2048]{1,0:T(8,128)(2,1)S(1)}, bf16[384,2048]{1,0:T(8,128)(2,1)}, u32[]{:S(2)}) copy-start(bf16[384,2048]{1,0:T(8,128)(2,1)} %copy-done) | copy-start | bytes 4718596
  172.9 21.6 %all-to-all-start.1 = ((bf16[8,48,1536]{2,1,0:T(8,128)(2,1)}), bf16[8,48,1536]{2,1,0:T(8,128)(2,1)S(1)}, u32[]{:S(2)}, u32[]{:S(2)}) async-start(bf16[8,48,1536]{2,1,0:T(8,128)(2,1)} %bitcast.53), calls=%async_computation.1 | async-start | bytes 2359296 | tf_op jit(solution)/shard_map/all_to_all | solution.py:75
  194.5 20.8 %all-to-all-start.3 = ((bf16[8,48,1536]{2,1,0:T(8,128)(2,1)}), bf16[8,48,1536]{2,1,0:T(8,128)(2,1)S(1)}, u32[]{:S(2)}, u32[]{:S(2)}) async-start(bf16[8,48,1536]{2,1,0:T(8,128)(2,1)} %bitcast.52), calls=%async_computation.3 | async-start | bytes 2359296 | tf_op jit(solution)/shard_map/all_to_all | solution.py:88
  219.7 5.1 %copy-start.4 = (f32[128,2]{1,0:T(8,128)S(1)}, f32[128,2]{1,0:T(8,128)}, u32[]{:S(2)}) copy-start(f32[128,2]{1,0:T(8,128)} %copy-done.3) | copy-start | bytes 3076
Sparse Core Ops, SparseCore 0:
  10.1 64.4 all-gather.2
  76.7 60.9 all-gather.4
  166.6 152.9 reduce-scatter.1
where the time goes:
time: 330 us
  waiting for transfers between devices  215 us (65%)
  matrix products  36.9 us (11%)
  other arithmetic  23 us (7%)
  local copies, waits for them, and re-layouts  21.4 us (6%)
  starting transfers between devices  20 us (6%)
  between operations  13.9 us (4%)
    reduce_scatter x1, waiting for transfers between devices, shards(): lax.psum_scatter(jnp.concatenate([contract_first(grad_hidden, recv_tokens...  90.7 us
    all_gather x1, waiting for transfers between devices, shards(): lax.all_gather(w_out, 'fsdp', axis=1, tiled=True)  55.6 us
    all_gather x1, waiting for transfers between devices, shards(): lax.all_gather(w_in, 'fsdp', axis=1, tiled=True)  31.6 us
    dot_general x2, matrix products, contract_last(): lax.dot_general(left, right, (((1,), (1,)), ((), ())), preferred_element_...  15.3 us
    all_to_all x1, waiting for transfers between devices, shards(): lax.all_to_all(input_grad, 'exp', split_axis=0, concat_axis=0, tiled=True)  14.2 us
    concatenate x1, other arithmetic, shards(): jnp.concatenate([contract_first(grad_hidden, recv_tokens), contract_first...  12.1 us
    all_to_all x1, waiting for transfers between devices, shards(): lax.all_to_all(send_tokens.reshape(groups, capacity, features), 'exp', sp...  11.2 us
    all_to_all x1, waiting for transfers between devices, shards(): lax.all_to_all(expert_out, 'exp', split_axis=0, concat_axis=0, tiled=True)  9.96 us
  transfers between devices with their start and end apart: 7, of which 6 were waited for; matrix products, arithmetic and copies ran while one was open for 15% of the time, Pallas kernels for 0%

commit v1 on v0

v1 whole, which is shorter than its diff:
```python
import functools

import jax
import jax.numpy as jnp
from jax import lax
from jax.experimental import pallas as pl
from jax.experimental.pallas import tpu as pltpu
from jax.sharding import PartitionSpec as P

inv_sqrt_two = 0.7071067811865476
inv_sqrt_two_pi = 0.3989422804014327
MESH = pl.DeviceIdType.MESH
SIDE = 4
BF = jnp.bfloat16
F32 = jnp.float32


def dot(left, right, over):
    return lax.dot_general(left, right, (over, ((), ())), preferred_element_type=F32)


def kernel(
    experts,
    ids_row,
    gates_row,
    gates_col,
    tokens,
    grad_y,
    w_in,
    w_out,
    mixed,
    grad_tokens,
    grad_in,
    grad_out,
    grad_gates,
    wts,
    parts,
    relay1,
    full1,
    relay2,
    full2,
    sendx,
    recvx,
    backx,
    acc,
    act_s,
    gh_s,
    act_t,
    gh_t,
    load_sem,
    ag_send,
    ag_recv,
    rs_send,
    rs_recv,
    x_send,
    x_recv,
):
    rows, features = tokens.shape
    half = w_in.shape[0] // 2
    cap = sendx.shape[2]
    slots = experts * cap
    group = SIDE * half
    tile = features // 3

    e = lax.axis_index("exp")
    f = lax.axis_index("fsdp")
    z, y = f // SIDE, f % SIDE

    def ring(value):
        return (value + SIDE) % SIDE

    first, second = (y, z), (z, y)

    def peer(h, second_axis, step):
        along_z = (h == 0) == second_axis
        nz = ring(z + step) if along_z else z
        ny = y if along_z else ring(y + step)
        return (e, nz * SIDE + ny)

    def copy(src, dst, send, recv, to):
        return pltpu.make_async_remote_copy(
            src_ref=src, dst_ref=dst, send_sem=send, recv_sem=recv, device_id=to, device_id_type=MESH
        )

    def gather_region(h, i, k, sent):
        a, b = first[h], second[h]
        if i is None:
            if sent:
                return (wts.at[h, a, b], wts.at[h, a, b], wts.at[h, ring(a - 1), b, 0], wts.at[h, ring(a + 1), b, 1])[k]
            return (
                wts.at[h, ring(a - 1), b],
                wts.at[h, ring(a + 1), b],
                wts.at[h, ring(a + 2), b, 0],
                wts.at[h, ring(a + 2), b, 1],
            )[k]
        g = ring(a - i)
        if sent:
            return (wts.at[h, g, b], wts.at[h, g, b], wts.at[h, g, ring(b - 1), 0], wts.at[h, g, ring(b + 1), 1])[k]
        return (
            wts.at[h, g, ring(b - 1)],
            wts.at[h, g, ring(b + 1)],
            wts.at[h, g, ring(b + 2), 0],
            wts.at[h, g, ring(b + 2), 1],
        )[k]

    def gather(h, i, k, sent=True):
        region = gather_region(h, i, k, sent)
        s = k if i is None else 4 + 4 * i + k
        step = 1 if k % 2 == 0 else -1
        return copy(region, region, ag_send.at[h, s], ag_recv.at[h, s], peer(h, i is not None, step))

    def got(h, i, k):
        gather(h, i, k, sent=False).wait_recv()

    def reduce1(h, i, k):
        a, b = first[h], second[h]
        g = ring(a - i)
        src = (
            parts.at[h, g, ring(b + 2), 0],
            parts.at[h, g, ring(b + 2), 1],
            parts.at[h, g, ring(b + 1)],
            parts.at[h, g, ring(b - 1)],
        )[k]
        dst = (relay1.at[h, i, 0], relay1.at[h, i, 1], full1.at[h, i, 0], full1.at[h, i, 1])[k]
        s = 4 + 4 * i + k
        return copy(src, dst, rs_send.at[h, s], rs_recv.at[h, s], peer(h, True, 1 if k % 2 == 0 else -1))

    def reduce2(h, k):
        a, b = first[h], second[h]
        src = (
            parts.at[h, ring(a + 2), b, 0],
            parts.at[h, ring(a + 2), b, 1],
            parts.at[h, ring(a + 1), b],
            parts.at[h, ring(a - 1), b],
        )[k]
        dst = (relay2.at[h, 0], relay2.at[h, 1], full2.at[h, 0], full2.at[h, 1])[k]
        return copy(src, dst, rs_send.at[h, k], rs_recv.at[h, k], peer(h, False, 1 if k % 2 == 0 else -1))

    def start_first(i):
        for h in (0, 1):
            reduce1(h, i, 0).start()
            reduce1(h, i, 1).start()

    def relay_first(i):
        for h in (0, 1):
            g = ring(first[h] - i)
            up, down = ring(second[h] + 1), ring(second[h] - 1)
            reduce1(h, i, 0).wait_recv()
            parts[h, g, up, 0] = (parts[h, g, up, 0].astype(F32) + relay1[h, i, 0].astype(F32)).astype(BF)
            reduce1(h, i, 1).wait_recv()
            parts[h, g, down, 1] = (parts[h, g, down, 1].astype(F32) + relay1[h, i, 1].astype(F32)).astype(BF)
        for h in (0, 1):
            reduce1(h, i, 2).start()
            reduce1(h, i, 3).start()

    def collect(h, i, part, more=None):
        g, b = ring(first[h] - i), second[h]
        total = parts[h, g, b, part].astype(F32) + full1[h, i, 0, part].astype(F32) + full1[h, i, 1, part].astype(F32)
        if more is not None:
            total = total + more.astype(F32)
        return total

    def wait_first(i):
        for h in (0, 1):
            reduce1(h, i, 2).wait_recv()
            reduce1(h, i, 3).wait_recv()

    def out_copy(step):
        to = (e + step) % experts
        return copy(sendx.at[to], recvx.at[e], x_send.at[0, step], x_recv.at[0, step], (to, f))

    def out_arrival(step):
        src = (e + experts - step) % experts
        return copy(sendx.at[src], recvx.at[src], x_send.at[0, step], x_recv.at[0, step], (src, f))

    def back_copy(step):
        to = (e + step) % experts
        return copy(sendx.at[to], backx.at[e], x_send.at[1, step], x_recv.at[1, step], (to, f))

    def back_arrival(step):
        src = (e + experts - step) % experts
        return copy(sendx.at[src], backx.at[src], x_send.at[1, step], x_recv.at[1, step], (src, f))

    loads = []
    for h in (0, 1):
        for k, w in ((0, w_in), (1, w_out)):
            loads.append(
                pltpu.make_async_copy(
                    w.at[pl.ds(h * half, half)], wts.at[h, first[h], second[h], k], load_sem.at[2 * h + k]
                )
            )
    for c in loads:
        c.start()
    barrier = pltpu.get_barrier_semaphore()
    for step in range(1, experts):
        pl.semaphore_signal(barrier, inc=1, device_id=((e + step) % experts, f), device_id_type=MESH)
    for h in (0, 1):
        for step in (1, -1):
            pl.semaphore_signal(barrier, inc=1, device_id=peer(h, False, step), device_id_type=MESH)
    for c in loads:
        c.wait()
    pl.semaphore_wait(barrier, experts + 3)

    for h in (0, 1):
        gather(h, None, 0).start()
        gather(h, None, 1).start()
    for h in (0, 1):
        gather(h, 0, 0).start()
        gather(h, 0, 1).start()

    lane = lax.broadcasted_iota(jnp.int32, (16, rows), 0)
    named = [(lane == ids_row[k : k + 1, :]).astype(F32) for k in (0, 1)]
    before = (
        lax.broadcasted_iota(jnp.int32, (rows, rows), 0) < lax.broadcasted_iota(jnp.int32, (rows, rows), 1)
    ).astype(BF)
    ahead = dot((named[0] + named[1]).astype(BF), before, ((1,), (0,)))
    slot = [
        ids_row[k : k + 1, :].astype(F32) * cap + jnp.sum(named[k] * ahead, axis=0, keepdims=True) for k in (0, 1)
    ]

    def chosen(k, start, count):
        at = lax.broadcasted_iota(jnp.int32, (count, rows), 0) + start
        return (at.astype(F32) == slot[k]).astype(F32)

    def fill(d, carry):
        pick = [chosen(k, d * cap, cap) for k in (0, 1)]
        either = (pick[0] + pick[1]).astype(BF)
        gate = jnp.sum(pick[0] * gates_row[0:1, :] + pick[1] * gates_row[1:2, :], axis=1, keepdims=True)
        sendx[d, 0] = dot(either, tokens[...], ((1,), (0,))).astype(BF)
        sendx[d, 1] = (dot(either, grad_y[...], ((1,), (0,))) * gate).astype(BF)
        return carry

    lax.fori_loop(0, experts, fill, 0)
    for step in range(1, experts):
        out_copy(step).start()
    recvx[e] = sendx[e]

    for h in (0, 1):
        got(h, None, 0)
        gather(h, None, 2).start()
        gather(h, 1, 0).start()
        gather(h, 1, 1).start()
        got(h, None, 1)
        gather(h, None, 3).start()
    for h in (0, 1):
        got(h, 0, 0)
        gather(h, 0, 2).start()
        got(h, 0, 1)
        gather(h, 0, 3).start()
    for h in (0, 1):
        got(h, None, 2)
        got(h, None, 3)
        gather(h, 2, 0).start()
        gather(h, 2, 1).start()
    for h in (0, 1):
        got(h, 1, 0)
        gather(h, 1, 2).start()
        got(h, 1, 1)
        gather(h, 1, 3).start()
    for h in (0, 1):
        gather(h, 3, 0).start()
        gather(h, 3, 1).start()
    for step in range(1, experts):
        out_arrival(step).wait_recv()
    for h in (0, 1):
        got(h, 0, 2)
        got(h, 0, 3)
    acc[...] = jnp.zeros_like(acc)

    def compute(it, carry):
        i, h = it // 2, it % 2

        @pl.when(it == 2)
        def _():
            for hh in (0, 1):
                got(hh, 2, 0)
                gather(hh, 2, 2).start()
                got(hh, 2, 1)
                gather(hh, 2, 3).start()
            for hh in (0, 1):
                got(hh, 1, 2)
                got(hh, 1, 3)

        @pl.when(it == 4)
        def _():
            for hh in (0, 1):
                got(hh, 3, 0)
                gather(hh, 3, 2).start()
                got(hh, 3, 1)
                gather(hh, 3, 3).start()
            start_first(1)
            start_first(0)
            for hh in (0, 1):
                got(hh, 2, 2)
                got(hh, 2, 3)

        @pl.when(it == 6)
        def _():
            start_first(2)
            relay_first(1)
            for hh in (0, 1):
                got(hh, 3, 2)
                got(hh, 3, 3)

        g = ring(y + h * (z - y) - i)

        def weight(k, *at):
            return wts[(h, g, slice(None), k, slice(None)) + at].reshape(group, -1)

        def patches(k, *at):
            return recvx[(slice(None), k, slice(None)) + at].reshape(slots, -1)

        pre = dot(patches(0), weight(0), ((1,), (1,)))
        grad_act = dot(patches(1), weight(1), ((1,), (1,)))
        cdf = 0.5 * (1.0 + lax.erf(pre * inv_sqrt_two))
        act = pre * cdf
        hidden = grad_act * (cdf + pre * jnp.exp(-0.5 * pre * pre) * inv_sqrt_two_pi)
        act_s[...] = act.astype(BF)
        gh_s[...] = hidden.astype(BF)
        act_t[...] = act.T.astype(BF)
        gh_t[...] = hidden.T.astype(BF)

        def columns(c, inner):
            at = pl.ds(pl.multiple_of(c * tile, tile), tile)
            acc[0, :, at] += dot(act_s[...], weight(1, at), ((1,), (0,)))
            acc[1, :, at] += dot(gh_s[...], weight(0, at), ((1,), (0,)))
            parts[h, g, :, 0, :, at] = dot(gh_t[...], patches(0, at), ((1,), (0,))).astype(BF).reshape(SIDE, half, tile)
            parts[h, g, :, 1, :, at] = dot(act_t[...], patches(1, at), ((1,), (0,))).astype(BF).reshape(SIDE, half, tile)
            return inner

        lax.fori_loop(0, 3, columns, 0)
        return carry

    lax.fori_loop(0, 8, compute, 0)

    start_first(3)
    for step in range(1, experts):
        out_copy(step).wait_send()
    for d in range(experts):
        for k in (0, 1):
            sendx[d, k] = acc[k, d * cap : (d + 1) * cap, :].astype(BF)
    relay_first(2)
    for step in range(1, experts):
        back_copy(step).start()
    backx[e] = sendx[e]

    relay_first(3)
    wait_first(2)
    for h in (0, 1):
        for part in (0, 1):
            parts[h, ring(first[h] + 2), second[h], part] = collect(h, 2, part).astype(BF)
    relay_first(0)
    for h in (0, 1):
        reduce2(h, 0).start()
        reduce2(h, 1).start()
    wait_first(1)
    wait_first(3)
    for h in (0, 1):
        reduce2(h, 0).wait_recv()
        reduce2(h, 1).wait_recv()
        up, down, b = ring(first[h] + 1), ring(first[h] - 1), second[h]
        parts[h, up, b, 0] = collect(h, 3, 0, relay2[h, 0]).astype(BF)
        parts[h, up, b, 1] = collect(h, 3, 1).astype(BF)
        parts[h, down, b, 0] = collect(h, 1, 0).astype(BF)
        parts[h, down, b, 1] = collect(h, 1, 1, relay2[h, 1]).astype(BF)
    for h in (0, 1):
        reduce2(h, 2).start()
        reduce2(h, 3).start()

    for step in range(1, experts):
        back_arrival(step).wait_recv()
    pick = [chosen(k, 0, slots).astype(BF) for k in (0, 1)]
    both = pick[0] + pick[1]
    by_gate = [jnp.zeros((rows, 1), F32) for _ in (0, 1)]
    for c in range(3):
        at = slice(c * tile, (c + 1) * tile)
        results = backx[:, 0, :, at].reshape(slots, tile)
        grads = backx[:, 1, :, at].reshape(slots, tile)
        cot = grad_y[:, at].astype(F32)
        total = jnp.zeros((rows, tile), F32)
        for k in (0, 1):
            one = dot(pick[k], results, ((0,), (0,)))
            total = total + gates_col[:, k : k + 1] * one
            by_gate[k] = by_gate[k] + jnp.sum(cot * one, axis=1, keepdims=True)
        mixed[:, at] = total.astype(BF)
        grad_tokens[:, at] = dot(both, grads, ((0,), (0,))).astype(BF)
    for k in (0, 1):
        grad_gates[:, k : k + 1] = by_gate[k]

    wait_first(0)
    for h in (0, 1):
        reduce2(h, 2).wait_recv()
        reduce2(h, 3).wait_recv()
        for part, out in ((0, grad_in), (1, grad_out)):
            total = collect(h, 0, part) + full2[h, 0, part].astype(F32) + full2[h, 1, part].astype(F32)
            out[h * half : (h + 1) * half, :] = total

    for step in range(1, experts):
        back_copy(step).wait_send()
    for h in (0, 1):
        for k in range(4):
            gather(h, None, k).wait_send()
            reduce2(h, k).wait_send()
            for i in range(SIDE):
                gather(h, i, k).wait_send()
                reduce1(h, i, k).wait_send()


def shards(tokens, expert_ids, gates, w_in, w_out, grad_y):
    rows, features = tokens.shape
    experts = lax.axis_size("exp")
    cap = 3 * rows // 8
    hidden = w_in.shape[1]
    half = hidden // 2
    group = SIDE * half
    slots = experts * cap
    vmem = pl.BlockSpec(memory_space=pltpu.VMEM)
    hbm = pl.BlockSpec(memory_space=pl.ANY)
    mixed, grad_tokens, grad_in, grad_out, grad_gates = pl.pallas_call(
        functools.partial(kernel, experts),
        name="moe",
        out_shape=(
            jax.ShapeDtypeStruct((rows, features), BF),
            jax.ShapeDtypeStruct((rows, features), BF),
            jax.ShapeDtypeStruct((hidden, features), F32),
            jax.ShapeDtypeStruct((hidden, features), F32),
            jax.ShapeDtypeStruct((rows, 2), F32),
        ),
        in_specs=[vmem] * 5 + [hbm] * 2,
        out_specs=(vmem,) * 5,
        scratch_shapes=[
            pltpu.VMEM((2, SIDE, SIDE, 2, half, features), BF),
            pltpu.VMEM((2, SIDE, SIDE, 2, half, features), BF),
            pltpu.VMEM((2, SIDE, 2, half, features), BF),
            pltpu.VMEM((2, SIDE, 2, 2, half, features), BF),
            pltpu.VMEM((2, 2, half, features), BF),
            pltpu.VMEM((2, 2, 2, half, features), BF),
            pltpu.VMEM((experts, 2, cap, features), BF),
            pltpu.VMEM((experts, 2, cap, features), BF),
            pltpu.VMEM((experts, 2, cap, features), BF),
            pltpu.VMEM((2, slots, features), F32),
            pltpu.VMEM((slots, group), BF),
            pltpu.VMEM((slots, group), BF),
            pltpu.VMEM((group, slots), BF),
            pltpu.VMEM((group, slots), BF),
            pltpu.SemaphoreType.DMA((4,)),
            pltpu.SemaphoreType.DMA((2, 20)),
            pltpu.SemaphoreType.DMA((2, 20)),
            pltpu.SemaphoreType.DMA((2, 20)),
            pltpu.SemaphoreType.DMA((2, 20)),
            pltpu.SemaphoreType.DMA((2, experts)),
            pltpu.SemaphoreType.DMA((2, experts)),
        ],
        compiler_params=pltpu.CompilerParams(
            collective_id=0, has_side_effects=True, vmem_limit_bytes=66_000_000
        ),
    )(expert_ids.T, gates.T, gates, tokens, grad_y, w_in[0], w_out[0])
    return mixed, grad_tokens, grad_in[None], grad_out[None], grad_gates


def solution(mesh):
    return jax.shard_map(
        shards,
        mesh=mesh,
        in_specs=(
            P(("exp", "fsdp"), None),
            P(("exp", "fsdp"), None),
            P(("exp", "fsdp"), None),
            P("exp", "fsdp", None),
            P("exp", "fsdp", None),
            P(("exp", "fsdp"), None),
        ),
        out_specs=(
            P(("exp", "fsdp"), None),
            P(("exp", "fsdp"), None),
            P("exp", "fsdp", None),
            P("exp", "fsdp", None),
            P(("exp", "fsdp"), None),
        ),
        check_vma=False,
    )
```

time: 330 us -> 153 us (0.46)
  waiting for transfers between devices: 215 us -> 0 us
  Pallas kernels: 0 us -> 144 us
  matrix products: 36.9 us -> 0 us
  other arithmetic: 23 us -> 0 us
  starting transfers between devices: 20 us -> 0 us
  local copies, waits for them, and re-layouts: 21.4 us -> 7.83 us
  between operations: 13.9 us -> 0.66 us
    pallas_call x0 -> x1, Pallas kernels: none -> 144 us  [shards(): pl.pallas_call(functools.partial(kernel, experts), name='moe', out_shape=...]
    reduce_scatter x1 -> x0, waiting for transfers between devices: 90.7 us -> none  [shards(): lax.psum_scatter(jnp.concatenate([contract_first(grad_hidden, recv_tokens...]
    all_gather x2 -> x0, waiting for transfers between devices: 87.2 us -> none  [the longest x1 55.6 us: shards(): lax.all_gather(w_out, 'fsdp', axis=1, tiled=True)]
    dot_general x6 -> x0, matrix products: 36.9 us -> none  [the longest x2 15.3 us: contract_last(): lax.dot_general(left, right, (((1,), (1,)), ((), ())), preferred_element_...]
    all_to_all x4 -> x0, waiting for transfers between devices: 35.4 us -> none  [the longest x1 14.2 us: shards(): lax.all_to_all(input_grad, 'exp', split_axis=0, concat_axis=0, tiled=True)]
    all_to_all x4 -> x0, starting transfers between devices: 19.9 us -> none  [the longest x1 5.79 us: shards(): lax.all_to_all(send_tokens.reshape(groups, capacity, features), 'exp', sp...]
    concatenate x1 -> x0, other arithmetic: 12.1 us -> none  [shards(): jnp.concatenate([contract_first(grad_hidden, recv_tokens), contract_first...]
    reduce_sum x3 -> x0, other arithmetic: 6.5 us -> none  [the longest x1 3.54 us: shards(): jnp.sum(grad_y.astype(jnp.float32)[:, None, :] * out_three, axis=-1)]
  transfers between devices with their start and end apart: 7 -> 0, of which waited for: 6 -> 0; matrix products, arithmetic and copies ran while one was open for 15% -> 0% of each run, Pallas kernels for 0% -> 0%
where the time goes in v1:
time: 153 us; the launch traced here: 152 us
  Pallas kernels  144 us (94%)
  local copies, waits for them, and re-layouts  7.83 us (5%)
    pallas_call x1, Pallas kernels, shards(): pl.pallas_call(functools.partial(kernel, experts), name='moe', out_shape=...  144 us
    unnamed x14, local copies, waits for them, and re-layouts  7.83 us

profile of v1, /device:TPU:1, one launch (start us, length us, event | category | flops | bytes accessed | tf_op | source)
XLA Modules:
  0.0 152.2 jit_solution(3473108571262015143)
XLA Ops:
  0.6 0.0 copy-start.3
  0.6 0.7 copy-done.3
  1.3 0.7 copy.11.gates_col
  2.1 143.7 %moe.1 = (bf16[128,1536]{1,0:T(8,128)(2,1)}, bf16[128,1536]{1,0:T(8,128)(2,1)}, f32[128,1536]{1,0:T(8,128)}, f32[128,1536]{1,0:T(8,128)}, f32[128,2]{1,0:T(8,128)}) custom-call(s32[2,128]{1,0:T(2,128)} %bitcast.11, f32[2,128]{1,0:T(2,128)} %bitcast.10, f32[128,2]{1,0:T(8,128)} %copy.11.gates_col, bf16[128,1536]{1,0:T(8,128)(2,1)} %tokens.1, ...), custom_call_target="tpu_custom_call" | custom-call | tf_op jit(solution)/shard_map/moe/pallas_call | solution.py:419
  145.8 0.0 copy-start.2
  145.8 1.5 %copy.12 = f32[128,2]{0,1:T(2,128)} copy(f32[128,2]{1,0:T(8,128)} %get-tuple-element.19) | data formatting | bytes 2048
  147.3 0.0 copy-start.1
  147.3 1.8 %copy.17 = bf16[128,1536]{1,0:T(8,128)(2,1)} copy(bf16[128,1536]{1,0:T(8,128)(2,1)} %get-tuple-element.25) | data formatting | bytes 786432
  149.2 0.0 copy-done.2
  149.2 0.7 copy.18
  149.9 0.0 copy-done.1
  149.9 0.0 copy-start
  149.9 0.9 copy.19
  150.8 0.5 copy-done
  151.3 0.9 copy.20
Async XLA Ops:
  0.6 0.7 copy-start.3
  145.8 3.4 %copy-start.2 = (bf16[128,1536]{1,0:T(8,128)(2,1)S(1)}, bf16[128,1536]{1,0:T(8,128)(2,1)}, u32[]{:S(2)}) copy-start(bf16[128,1536]{1,0:T(8,128)(2,1)} %get-tuple-element.26) | copy-start | bytes 1179652
  147.3 2.6 %copy-start.1 = (f32[128,1536]{1,0:T(8,128)S(1)}, f32[128,1536]{1,0:T(8,128)}, u32[]{:S(2)}) copy-start(f32[128,1536]{1,0:T(8,128)} %get-tuple-element.12) | copy-start | bytes 2359300
  149.9 1.4 copy-start

commit v2 on v1

--- a/solution.py
+++ b/solution.py
@@ -23,7 +23,6 @@
     experts,
     ids_row,
     gates_row,
-    gates_col,
     tokens,
     grad_y,
     w_in,
@@ -371,6 +370,11 @@
         back_arrival(step).wait_recv()
     pick = [chosen(k, 0, slots).astype(BF) for k in (0, 1)]
     both = pick[0] + pick[1]
+    square = (rows, rows)
+    diagonal = (
+        lax.broadcasted_iota(jnp.int32, square, 0) == lax.broadcasted_iota(jnp.int32, square, 1)
+    ).astype(F32)
+    gate_col = [jnp.sum(diagonal * gates_row[k : k + 1, :], axis=1, keepdims=True) for k in (0, 1)]
     by_gate = [jnp.zeros((rows, 1), F32) for _ in (0, 1)]
     for c in range(3):
         at = slice(c * tile, (c + 1) * tile)
@@ -380,12 +384,12 @@
         total = jnp.zeros((rows, tile), F32)
         for k in (0, 1):
             one = dot(pick[k], results, ((0,), (0,)))
-            total = total + gates_col[:, k : k + 1] * one
+            total = total + gate_col[k] * one
             by_gate[k] = by_gate[k] + jnp.sum(cot * one, axis=1, keepdims=True)
         mixed[:, at] = total.astype(BF)
         grad_tokens[:, at] = dot(both, grads, ((0,), (0,))).astype(BF)
     for k in (0, 1):
-        grad_gates[:, k : k + 1] = by_gate[k]
+        grad_gates[k : k + 1, :] = jnp.sum(diagonal * by_gate[k], axis=0, keepdims=True)
 
     wait_first(0)
     for h in (0, 1):
@@ -404,6 +408,19 @@
             for i in range(SIDE):
                 gather(h, i, k).wait_send()
                 reduce1(h, i, k).wait_send()
+
+
+def place(*refs):
+    given, taken, held, (into, outof) = refs[:5], refs[5:10], refs[10:15], refs[15:]
+    ins = [pltpu.make_async_copy(given[k], held[k], into.at[k]) for k in range(5)]
+    outs = [pltpu.make_async_copy(held[k], taken[k], outof.at[k]) for k in range(5)]
+    for c in ins:
+        c.start()
+    for k in range(5):
+        ins[k].wait()
+        outs[k].start()
+    for c in outs:
+        c.wait()
 
 
 def shards(tokens, expert_ids, gates, w_in, w_out, grad_y):
@@ -424,9 +441,9 @@
             jax.ShapeDtypeStruct((rows, features), BF),
             jax.ShapeDtypeStruct((hidden, features), F32),
             jax.ShapeDtypeStruct((hidden, features), F32),
-            jax.ShapeDtypeStruct((rows, 2), F32),
+            jax.ShapeDtypeStruct((2, rows), F32),
         ),
-        in_specs=[vmem] * 5 + [hbm] * 2,
+        in_specs=[vmem] * 4 + [hbm] * 2,
         out_specs=(vmem,) * 5,
         scratch_shapes=[
             pltpu.VMEM((2, SIDE, SIDE, 2, half, features), BF),
@@ -454,8 +471,18 @@
         compiler_params=pltpu.CompilerParams(
             collective_id=0, has_side_effects=True, vmem_limit_bytes=66_000_000
         ),
-    )(expert_ids.T, gates.T, gates, tokens, grad_y, w_in[0], w_out[0])
-    return mixed, grad_tokens, grad_in[None], grad_out[None], grad_gates
+    )(expert_ids.T, gates.T, tokens, grad_y, w_in[0], w_out[0])
+    results = (grad_in, grad_out, mixed, grad_tokens, grad_gates)
+    grad_in, grad_out, mixed, grad_tokens, grad_gates = pl.pallas_call(
+        place,
+        name="place",
+        out_shape=tuple(jax.ShapeDtypeStruct(r.shape, r.dtype) for r in results),
+        in_specs=[hbm] * 5,
+        out_specs=(hbm,) * 5,
+        scratch_shapes=[pltpu.VMEM(r.shape, r.dtype) for r in results]
+        + [pltpu.SemaphoreType.DMA((5,)), pltpu.SemaphoreType.DMA((5,))],
+    )(*results)
+    return mixed, grad_tokens, grad_in[None], grad_out[None], grad_gates.T
 
 
 def solution(mesh):

time: 153 us -> 147 us (0.961)
  local copies, waits for them, and re-layouts: 7.83 us -> 0 us
  Pallas kernels: 144 us -> 146 us
    unnamed x14 -> x0, local copies, waits for them, and re-layouts: 7.83 us -> none
    pallas_call x0 -> x1, Pallas kernels: none -> 2.62 us  [shards(): pl.pallas_call(place, name='place', out_shape=tuple((jax.ShapeDtypeStruct...]
where the time goes in v2:
time: 147 us
  Pallas kernels  146 us (99%)
    pallas_call x1, Pallas kernels, shards(): pl.pallas_call(functools.partial(kernel, experts), name='moe', out_shape=...  144 us

profile of v2, /device:TPU:1, one launch (start us, length us, event | category | flops | bytes accessed | tf_op | source)
XLA Modules:
  0.0 147.0 jit_solution(12034125154200867026)
XLA Ops:
  0.6 143.7 %moe.1 = (bf16[128,1536]{1,0:T(8,128)(2,1)}, bf16[128,1536]{1,0:T(8,128)(2,1)}, f32[128,1536]{1,0:T(8,128)}, f32[128,1536]{1,0:T(8,128)}, f32[2,128]{1,0:T(2,128)}) custom-call(s32[2,128]{1,0:T(2,128)} %bitcast.9, f32[2,128]{1,0:T(2,128)} %bitcast.10, bf16[128,1536]{1,0:T(8,128)(2,1)} %tokens.1, bf16[128,1536]{1,0:T(8,128)(2,1)} %grad_y.1, ...), custom_call_target="tpu_custom_call" | custom-call | tf_op jit(solution)/shard_map/moe/pallas_call | solution.py:436
  144.4 2.6 %place.1 = (f32[128,1536]{1,0:T(8,128)}, f32[128,1536]{1,0:T(8,128)}, bf16[128,1536]{1,0:T(8,128)(2,1)}, bf16[128,1536]{1,0:T(8,128)(2,1)}, f32[2,128]{1,0:T(2,128)}) custom-call(f32[128,1536]{1,0:T(8,128)} %get-tuple-element.15.refs_0_, f32[128,1536]{1,0:T(8,128)} %get-tuple-element.16.refs_1_, bf16[128,1536]{1,0:T(8,128)(2,1)} %get-tuple-element.17.refs_2_, ...), custom_call_target="tpu_custom_call" | custom-call | tf_op jit(solution)/shard_map/place/pallas_call | solution.py:476

commit v3 on v2

v3 whole, which is shorter than its diff:
```python
import functools

import jax
import jax.numpy as jnp
from jax import lax
from jax.experimental import pallas as pl
from jax.experimental.pallas import tpu as pltpu
from jax.sharding import PartitionSpec as P

inv_sqrt_two = 0.7071067811865476
inv_sqrt_two_pi = 0.3989422804014327
MESH = pl.DeviceIdType.MESH
SIDE = 4
BF = jnp.bfloat16
F32 = jnp.float32


def dot(left, right, over):
    return lax.dot_general(left, right, (over, ((), ())), preferred_element_type=F32)


def kernel(
    experts,
    ids_row,
    gates_row,
    tokens,
    grad_y,
    w_in,
    w_out,
    mixed,
    grad_tokens,
    grad_in,
    grad_out,
    grad_gates,
    wts,
    parts0,
    parts1,
    relay0,
    full0,
    last0,
    mate1,
    relay1,
    full1,
    raw_tokens,
    raw_grads,
    raw_ids,
    raw_gates,
    sendx,
    recvx,
    backx,
    acc,
    act_s,
    gh_s,
    act_t,
    gh_t,
    load_sem,
    raw_send,
    raw_recv,
    ag_send,
    ag_recv,
    rs_send,
    rs_recv,
    x_send,
    x_recv,
):
    rows, features = tokens.shape
    half = w_in.shape[0] // 2
    cap = sendx.shape[3]
    slots = experts * cap
    group = SIDE * half
    tile = features // 3

    e = lax.axis_index("exp")
    f = lax.axis_index("fsdp")
    z, y = f // SIDE, f % SIDE
    odd = y % 2
    side = y // 2
    toward = 1 - 2 * odd

    def ring(value):
        return (value + SIDE) % SIDE

    first, second = (y, z), (z, y)

    def axis_of(h, i):
        return "yz"[(h + (i is not None)) % 2]

    def step_of(axis, k):
        if axis == "z":
            return 1 if k % 2 == 0 else -1
        return toward if k % 2 == 0 else -toward

    def peer(axis, k):
        step = step_of(axis, k)
        return (e, ring(z + step) * SIDE + y if axis == "z" else z * SIDE + ring(y + step))

    def copy(src, dst, send, recv, to):
        return pltpu.make_async_remote_copy(
            src_ref=src, dst_ref=dst, send_sem=send, recv_sem=recv, device_id=to, device_id_type=MESH
        )

    def held(h, i):
        return ring(y + toward * i) if h == 0 else ring(z - i)

    def weights(h, i, offset, part=None):
        if i is None:
            at = (h, ring(first[h] + offset), second[h])
        else:
            at = (h, held(h, i), ring(second[h] + offset))
        return wts.at[at if part is None else at + (part,)]

    def gather(h, i, k):
        axis = axis_of(h, i)
        region = weights(h, i, 0) if k < 2 else weights(h, i, -step_of(axis, k), k - 2)
        s = k if i is None else 4 + 4 * i + k
        return copy(region, region, ag_send.at[h, s], ag_recv.at[h, s], peer(axis, k))

    def got(h, i, k):
        axis = axis_of(h, i)
        if k < 2:
            region = weights(h, i, -step_of(axis, k) if axis == "z" else step_of(axis, k))
        else:
            region = weights(h, i, 2, k - 2)
        s = k if i is None else 4 + 4 * i + k
        copy(region, region, ag_send.at[h, s], ag_recv.at[h, s], peer(axis, k)).wait_recv()

    def send(h, i):
        gather(h, i, 0).start()
        gather(h, i, 1).start()

    def forward(h, i, k):
        got(h, i, k - 2 if axis_of(h, i) == "z" else 3 - k)
        gather(h, i, k).start()

    def whole(h, i):
        got(h, i, 2)
        got(h, i, 3)

    raws = [
        copy(src, dst, raw_send.at[k], raw_recv.at[k], peer("y", 1))
        for k, (src, dst) in enumerate(
            ((ids_row, raw_ids), (gates_row, raw_gates), (tokens, raw_tokens), (grad_y, raw_grads))
        )
    ]

    def out_copy(line, step):
        to = (e + step) % experts
        return copy(sendx.at[line, to], recvx.at[line, e], x_send.at[line, step], x_recv.at[line, step], (to, f))

    def out_arrival(line, step):
        src = (e + experts - step) % experts
        return copy(sendx.at[line, src], recvx.at[line, src], x_send.at[line, step], x_recv.at[line, step], (src, f))

    def back_copy(step):
        to = (e + step) % experts
        return copy(sendx.at[0, to], backx.at[e], x_send.at[2, step], x_recv.at[2, step], (to, f))

    def back_arrival(step):
        src = (e + experts - step) % experts
        return copy(sendx.at[0, src], backx.at[src], x_send.at[2, step], x_recv.at[2, step], (src, f))

    def ring0(j, k):
        src = (
            parts0.at[j, ring(z + 2), 0],
            parts0.at[j, ring(z + 2), 1],
            parts0.at[j, ring(z + 1)],
            parts0.at[j, ring(z - 1)],
        )[k]
        dst = (relay0.at[j, 0], relay0.at[j, 1], full0.at[j, 0], full0.at[j, 1])[k]
        return copy(src, dst, rs_send.at[0, 4 * j + k], rs_recv.at[0, 4 * j + k], peer("z", k))

    def mate0():
        return copy(parts0.at[1, z], last0, rs_send.at[0, 8], rs_recv.at[0, 8], peer("y", 0))

    def to_mate1(i):
        return copy(parts1.at[i, 1 - odd], mate1.at[i], rs_send.at[1, i], rs_recv.at[1, i], peer("y", 0))

    def ring1(k):
        src = (parts1.at[2, odd, 0], parts1.at[2, odd, 1], parts1.at[3, odd], parts1.at[1, odd])[k]
        dst = (relay1.at[0], relay1.at[1], full1.at[0], full1.at[1])[k]
        return copy(src, dst, rs_send.at[1, 4 + k], rs_recv.at[1, 4 + k], peer("z", k))

    def add(*terms):
        total = terms[0].astype(F32)
        for t in terms[1:]:
            total = total + t.astype(F32)
        return total

    def relay_ring0(j):
        up, down = ring(z + 1), ring(z - 1)
        ring0(j, 0).wait_recv()
        parts0[j, up, 0] = add(parts0[j, up, 0], relay0[j, 0]).astype(BF)
        ring0(j, 1).wait_recv()
        parts0[j, down, 1] = add(parts0[j, down, 1], relay0[j, 1]).astype(BF)
        ring0(j, 2).start()
        ring0(j, 3).start()

    loads = []
    for h in (0, 1):
        for k, w in ((0, w_in), (1, w_out)):
            loads.append(
                pltpu.make_async_copy(
                    w.at[pl.ds(h * half, half)], wts.at[h, first[h], second[h], k], load_sem.at[2 * h + k]
                )
            )
    for c in loads:
        c.start()
    barrier = pltpu.get_barrier_semaphore()
    for step in range(1, experts):
        pl.semaphore_signal(barrier, inc=1, device_id=((e + step) % experts, f), device_id_type=MESH)
    for axis in "yz":
        for k in (0, 1):
            pl.semaphore_signal(barrier, inc=1, device_id=peer(axis, k), device_id_type=MESH)
    for c in loads:
        c.wait()
    pl.semaphore_wait(barrier, experts + 3)

    send(0, None)
    for c in raws:
        c.start()
    send(1, None)
    send(0, 0)
    send(1, 0)

    def slots_of(ids):
        lane = lax.broadcasted_iota(jnp.int32, (16, rows), 0)
        named = [(lane == ids[k : k + 1, :]).astype(F32) for k in (0, 1)]
        before = (
            lax.broadcasted_iota(jnp.int32, (rows, rows), 0) < lax.broadcasted_iota(jnp.int32, (rows, rows), 1)
        ).astype(BF)
        ahead = dot((named[0] + named[1]).astype(BF), before, ((1,), (0,)))
        return [
            ids[k : k + 1, :].astype(F32) * cap + jnp.sum(named[k] * ahead, axis=0, keepdims=True) for k in (0, 1)
        ]

    def chosen(slot, start, count):
        at = lax.broadcasted_iota(jnp.int32, (count, rows), 0) + start
        return (at.astype(F32) == slot).astype(F32)

    def dispatch(line, ids, gates, patch, cotangent):
        slot = slots_of(ids)

        def fill(d, carry):
            pick = [chosen(slot[k], d * cap, cap) for k in (0, 1)]
            either = (pick[0] + pick[1]).astype(BF)
            gate = jnp.sum(pick[0] * gates[0:1, :] + pick[1] * gates[1:2, :], axis=1, keepdims=True)
            sendx[line, d, 0] = dot(either, patch[...], ((1,), (0,))).astype(BF)
            sendx[line, d, 1] = (dot(either, cotangent[...], ((1,), (0,))) * gate).astype(BF)
            return carry

        lax.fori_loop(0, experts, fill, 0)
        for step in range(1, experts):
            out_copy(line, step).start()
        recvx[line, e] = sendx[line, e]

    dispatch(0, ids_row, gates_row, tokens, grad_y)

    forward(0, None, 3)
    send(0, 1)
    forward(0, None, 2)
    send(0, 3)
    forward(1, None, 2)
    send(1, 1)
    forward(1, None, 3)
    send(1, 3)
    forward(0, 0, 2)
    forward(0, 0, 3)
    forward(1, 0, 3)
    whole(1, None)
    send(1, 2)
    for c in raws:
        c.wait_recv()
    dispatch(1, raw_ids, raw_gates, raw_tokens, raw_grads)
    forward(0, 1, 2)
    forward(0, 1, 3)
    whole(0, None)
    send(0, 2)
    forward(0, 3, 2)
    forward(0, 3, 3)
    acc[...] = jnp.zeros_like(acc)
    for step in range(1, experts):
        out_arrival(0, step).wait_recv()

    def gelu(pre):
        cdf = 0.5 * (1.0 + lax.erf(pre * inv_sqrt_two))
        return pre * cdf, cdf + pre * jnp.exp(-0.5 * pre * pre) * inv_sqrt_two_pi

    def results(h, i):
        g = (1 - h) * ring(y + toward * i) + h * ring(z - i)

        def weight(k, *at):
            return wts[(h, g, slice(None), k, slice(None)) + at].reshape(group, -1)

        def patches(k):
            return recvx[0, :, k].reshape(slots, features)

        act, slope = gelu(dot(patches(0), weight(0), ((1,), (1,))))
        act_s[...] = act.astype(BF)
        gh_s[...] = (dot(patches(1), weight(1), ((1,), (1,))) * slope).astype(BF)

        def columns(c, inner):
            at = pl.ds(pl.multiple_of(c * tile, tile), tile)
            acc[0, :, at] += dot(act_s[...], weight(1, at), ((1,), (0,)))
            acc[1, :, at] += dot(gh_s[...], weight(0, at), ((1,), (0,)))
            return inner

        lax.fori_loop(0, 3, columns, 0)

    def gradients(h, q):
        def weight(k, at):
            if h == 0:
                return wts[0, held(0, q), :, k, :, at].reshape(group, -1)
            pair = [wts[1, held(1, i), pl.ds(2 * side, 2), k, :, at].reshape(group // 2, -1) for i in (q, q + 1)]
            return jnp.concatenate(pair, axis=0)

        every = slice(None)

        def line_of(line, inner):
            act, slope = gelu(dot(recvx[line, :, 0].reshape(slots, features), weight(0, every), ((1,), (1,))))
            hidden = dot(recvx[line, :, 1].reshape(slots, features), weight(1, every), ((1,), (1,))) * slope
            at = pl.ds(pl.multiple_of(line * slots, slots), slots)
            act_t[:, at] = act.T.astype(BF)
            gh_t[:, at] = hidden.T.astype(BF)
            return inner

        lax.fori_loop(0, 2, line_of, 0)

        def columns(c, inner):
            at = pl.ds(pl.multiple_of(c * tile, tile), tile)
            for k, left in ((0, gh_t), (1, act_t)):
                part = dot(left[...], recvx[:, :, k, :, at].reshape(2 * slots, tile), ((1,), (0,))).astype(BF)
                if h == 0:
                    parts0[q, :, k, :, at] = part.reshape(SIDE, half, tile)
                else:
                    parts1[pl.ds(q, 2), :, k, :, at] = part.reshape(2, 2, half, tile)
            return inner

        lax.fori_loop(0, 3, columns, 0)

    def first_results(it, power):
        @pl.when(it == 0)
        def _():
            whole(0, 0)

        @pl.when(it == 1)
        def _():
            forward(1, 0, 2)
            whole(0, 1)

        @pl.when(it == 2)
        def _():
            forward(1, 1, 3)
            forward(0, 2, 2)
            forward(0, 2, 3)
            whole(0, 3)

        results(0, (0o310 // power) % 8)
        return power * 8

    lax.fori_loop(0, 3, first_results, 1)

    forward(1, 1, 2)
    forward(1, 3, 3)
    forward(1, 2, 3)
    for step in range(1, experts):
        out_arrival(1, step).wait_recv()
    gradients(1, 2)
    to_mate1(2).start()
    to_mate1(3).start()
    forward(1, 3, 2)
    gradients(1, 0)
    to_mate1(1).start()
    to_mate1(0).start()
    gradients(0, 1)
    ring0(1, 0).start()
    ring0(1, 1).start()
    gradients(0, 0)
    ring0(0, 0).start()
    ring0(0, 1).start()
    forward(1, 2, 2)

    def last_results(it, power):
        @pl.when(it == 0)
        def _():
            whole(0, 2)
            to_mate1(2).wait_recv()
            parts1[2, odd] = add(parts1[2, odd], mate1[2]).astype(BF)

        @pl.when(it == 1)
        def _():
            ring1(0).start()
            ring1(1).start()
            relay_ring0(1)
            whole(1, 0)

        @pl.when(it == 2)
        def _():
            relay_ring0(0)
            whole(1, 1)

        @pl.when(it == 3)
        def _():
            whole(1, 3)

        @pl.when(it == 4)
        def _():
            whole(1, 2)

        results((0o11110 // power) % 8, (0o23102 // power) % 8)
        return power * 8

    lax.fori_loop(0, 5, last_results, 1)

    for step in range(1, experts):
        out_copy(0, step).wait_send()
    for d in range(experts):
        for k in (0, 1):
            sendx[0, d, k] = acc[k, d * cap : (d + 1) * cap, :].astype(BF)
    for step in range(1, experts):
        back_copy(step).start()
    backx[e] = sendx[0, e]

    to_mate1(3).wait_recv()
    to_mate1(1).wait_recv()
    ring1(0).wait_recv()
    ring1(1).wait_recv()
    parts1[3, odd, 0] = add(parts1[3, odd, 0], mate1[3, 0], relay1[0]).astype(BF)
    parts1[3, odd, 1] = add(parts1[3, odd, 1], mate1[3, 1]).astype(BF)
    parts1[1, odd, 0] = add(parts1[1, odd, 0], mate1[1, 0]).astype(BF)
    parts1[1, odd, 1] = add(parts1[1, odd, 1], mate1[1, 1], relay1[1]).astype(BF)
    ring1(2).start()
    ring1(3).start()
    ring0(1, 2).wait_recv()
    ring0(1, 3).wait_recv()
    parts0[1, z] = add(parts0[1, z], full0[1, 0], full0[1, 1]).astype(BF)
    mate0().start()

    to_mate1(0).wait_recv()
    ring1(2).wait_recv()
    ring1(3).wait_recv()
    for part, out in ((0, grad_in), (1, grad_out)):
        out[half : 2 * half, :] = add(
            parts1[0, odd, part], mate1[0, part], full1[0, part], full1[1, part]
        )
    ring0(0, 2).wait_recv()
    ring0(0, 3).wait_recv()
    mate0().wait_recv()
    for part, out in ((0, grad_in), (1, grad_out)):
        out[0:half, :] = add(parts0[0, z, part], full0[0, 0, part], full0[0, 1, part], last0[part])

    for step in range(1, experts):
        back_arrival(step).wait_recv()
    slot = slots_of(ids_row)
    pick = [chosen(slot[k], 0, slots).astype(BF) for k in (0, 1)]
    both = pick[0] + pick[1]
    square = (rows, rows)
    diagonal = (
        lax.broadcasted_iota(jnp.int32, square, 0) == lax.broadcasted_iota(jnp.int32, square, 1)
    ).astype(F32)
    gate_col = [jnp.sum(diagonal * gates_row[k : k + 1, :], axis=1, keepdims=True) for k in (0, 1)]
    by_gate = [jnp.zeros((rows, 1), F32) for _ in (0, 1)]
    for c in range(3):
        at = slice(c * tile, (c + 1) * tile)
        outs = backx[:, 0, :, at].reshape(slots, tile)
        grads = backx[:, 1, :, at].reshape(slots, tile)
        cot = grad_y[:, at].astype(F32)
        total = jnp.zeros((rows, tile), F32)
        for k in (0, 1):
            one = dot(pick[k], outs, ((0,), (0,)))
            total = total + gate_col[k] * one
            by_gate[k] = by_gate[k] + jnp.sum(cot * one, axis=1, keepdims=True)
        mixed[:, at] = total.astype(BF)
        grad_tokens[:, at] = dot(both, grads, ((0,), (0,))).astype(BF)
    for k in (0, 1):
        grad_gates[k : k + 1, :] = jnp.sum(diagonal * by_gate[k], axis=0, keepdims=True)

    for c in raws:
        c.wait_send()
    for step in range(1, experts):
        out_copy(1, step).wait_send()
        back_copy(step).wait_send()
    mate0().wait_send()
    for k in range(4):
        to_mate1(k).wait_send()
        ring1(k).wait_send()
        for j in (0, 1):
            ring0(j, k).wait_send()
        for h in (0, 1):
            for i in (None, 0, 1, 2, 3):
                gather(h, i, k).wait_send()


def place(*refs):
    given, taken, held, (into, outof) = refs[:5], refs[5:10], refs[10:15], refs[15:]
    ins = [pltpu.make_async_copy(given[k], held[k], into.at[k]) for k in range(5)]
    outs = [pltpu.make_async_copy(held[k], taken[k], outof.at[k]) for k in range(5)]
    for c in ins:
        c.start()
    for k in range(5):
        ins[k].wait()
        outs[k].start()
    for c in outs:
        c.wait()


def shards(tokens, expert_ids, gates, w_in, w_out, grad_y):
    rows, features = tokens.shape
    experts = lax.axis_size("exp")
    cap = 3 * rows // 8
    hidden = w_in.shape[1]
    half = hidden // 2
    group = SIDE * half
    slots = experts * cap
    vmem = pl.BlockSpec(memory_space=pltpu.VMEM)
    hbm = pl.BlockSpec(memory_space=pl.ANY)
    mixed, grad_tokens, grad_in, grad_out, grad_gates = pl.pallas_call(
        functools.partial(kernel, experts),
        name="moe",
        out_shape=(
            jax.ShapeDtypeStruct((rows, features), BF),
            jax.ShapeDtypeStruct((rows, features), BF),
            jax.ShapeDtypeStruct((hidden, features), F32),
            jax.ShapeDtypeStruct((hidden, features), F32),
            jax.ShapeDtypeStruct((2, rows), F32),
        ),
        in_specs=[vmem] * 4 + [hbm] * 2,
        out_specs=(vmem,) * 5,
        scratch_shapes=[
            pltpu.VMEM((2, SIDE, SIDE, 2, half, features), BF),
            pltpu.VMEM((2, SIDE, 2, half, features), BF),
            pltpu.VMEM((SIDE, 2, 2, half, features), BF),
            pltpu.VMEM((2, 2, half, features), BF),
            pltpu.VMEM((2, 2, 2, half, features), BF),
            pltpu.VMEM((2, half, features), BF),
            pltpu.VMEM((SIDE, 2, half, features), BF),
            pltpu.VMEM((2, half, features), BF),
            pltpu.VMEM((2, 2, half, features), BF),
            pltpu.VMEM((rows, features), BF),
            pltpu.VMEM((rows, features), BF),
            pltpu.VMEM((2, rows), jnp.int32),
            pltpu.VMEM((2, rows), F32),
            pltpu.VMEM((2, experts, 2, cap, features), BF),
            pltpu.VMEM((2, experts, 2, cap, features), BF),
            pltpu.VMEM((experts, 2, cap, features), BF),
            pltpu.VMEM((2, slots, features), F32),
            pltpu.VMEM((slots, group), BF),
            pltpu.VMEM((slots, group), BF),
            pltpu.VMEM((group, 2 * slots), BF),
            pltpu.VMEM((group, 2 * slots), BF),
            pltpu.SemaphoreType.DMA((4,)),
            pltpu.SemaphoreType.DMA((4,)),
            pltpu.SemaphoreType.DMA((4,)),
            pltpu.SemaphoreType.DMA((2, 20)),
            pltpu.SemaphoreType.DMA((2, 20)),
            pltpu.SemaphoreType.DMA((2, 9)),
            pltpu.SemaphoreType.DMA((2, 9)),
            pltpu.SemaphoreType.DMA((3, experts)),
            pltpu.SemaphoreType.DMA((3, experts)),
        ],
        compiler_params=pltpu.CompilerParams(
            collective_id=0, has_side_effects=True, vmem_limit_bytes=66_000_000
        ),
    )(expert_ids.T, gates.T, tokens, grad_y, w_in[0], w_out[0])
    results = (grad_in, grad_out, mixed, grad_tokens, grad_gates)
    grad_in, grad_out, mixed, grad_tokens, grad_gates = pl.pallas_call(
        place,
        name="place",
        out_shape=tuple(jax.ShapeDtypeStruct(r.shape, r.dtype) for r in results),
        in_specs=[hbm] * 5,
        out_specs=(hbm,) * 5,
        scratch_shapes=[pltpu.VMEM(r.shape, r.dtype) for r in results]
        + [pltpu.SemaphoreType.DMA((5,)), pltpu.SemaphoreType.DMA((5,))],
    )(*results)
    return mixed, grad_tokens, grad_in[None], grad_out[None], grad_gates.T


def solution(mesh):
    return jax.shard_map(
        shards,
        mesh=mesh,
        in_specs=(
            P(("exp", "fsdp"), None),
            P(("exp", "fsdp"), None),
            P(("exp", "fsdp"), None),
            P("exp", "fsdp", None),
            P("exp", "fsdp", None),
            P(("exp", "fsdp"), None),
        ),
        out_specs=(
            P(("exp", "fsdp"), None),
            P(("exp", "fsdp"), None),
            P("exp", "fsdp", None),
            P("exp", "fsdp", None),
            P(("exp", "fsdp"), None),
        ),
        check_vma=False,
    )
```

time: 147 us -> 157 us (1.068)
  Pallas kernels: 146 us -> 156 us
    pallas_call x1, Pallas kernels: 144 us -> 153 us  [shards(): pl.pallas_call(functools.partial(kernel, experts), name='moe', out_shape=...]
where the time goes in v3:
time: 157 us; the launch traced here: 156 us
  Pallas kernels  156 us (99%)
    pallas_call x1, Pallas kernels, shards(): pl.pallas_call(functools.partial(kernel, experts), name='moe', out_shape=...  153 us

profile of v3, /device:TPU:1, one launch (start us, length us, event | category | flops | bytes accessed | tf_op | source)
XLA Modules:
  0.0 156.5 jit_solution(6589339806410744931)
XLA Ops:
  0.6 153.2 %moe.1 = (bf16[128,1536]{1,0:T(8,128)(2,1)}, bf16[128,1536]{1,0:T(8,128)(2,1)}, f32[128,1536]{1,0:T(8,128)}, f32[128,1536]{1,0:T(8,128)}, f32[2,128]{1,0:T(2,128)}) custom-call(s32[2,128]{1,0:T(2,128)} %bitcast.9, f32[2,128]{1,0:T(2,128)} %bitcast.10, bf16[128,1536]{1,0:T(8,128)(2,1)} %tokens.1, bf16[128,1536]{1,0:T(8,128)(2,1)} %grad_y.1, ...), custom_call_target="tpu_custom_call" | custom-call | tf_op jit(solution)/shard_map/moe/pallas_call | solution.py:516
  153.9 2.6 %place.1 = (f32[128,1536]{1,0:T(8,128)}, f32[128,1536]{1,0:T(8,128)}, bf16[128,1536]{1,0:T(8,128)(2,1)}, bf16[128,1536]{1,0:T(8,128)(2,1)}, f32[2,128]{1,0:T(2,128)}) custom-call(f32[128,1536]{1,0:T(8,128)} %get-tuple-element.15.refs_0_, f32[128,1536]{1,0:T(8,128)} %get-tuple-element.16.refs_1_, bf16[128,1536]{1,0:T(8,128)(2,1)} %get-tuple-element.17.refs_2_, ...), custom_call_target="tpu_custom_call" | custom-call | tf_op jit(solution)/shard_map/place/pallas_call | solution.py:565

commit v4 on v3

--- a/solution.py
+++ b/solution.py
@@ -364,20 +364,20 @@
     forward(1, 2, 3)
     for step in range(1, experts):
         out_arrival(1, step).wait_recv()
+    forward(1, 3, 2)
     gradients(1, 2)
     to_mate1(2).start()
     to_mate1(3).start()
-    forward(1, 3, 2)
     gradients(1, 0)
-    to_mate1(1).start()
-    to_mate1(0).start()
     gradients(0, 1)
     ring0(1, 0).start()
     ring0(1, 1).start()
+    forward(1, 2, 2)
+    to_mate1(1).start()
+    to_mate1(0).start()
     gradients(0, 0)
     ring0(0, 0).start()
     ring0(0, 1).start()
-    forward(1, 2, 2)
 
     def last_results(it, power):
         @pl.when(it == 0)

time: 157 us -> 140 us (0.89)
  Pallas kernels: 156 us -> 139 us
    pallas_call x1, Pallas kernels: 153 us -> 136 us  [shards(): pl.pallas_call(functools.partial(kernel, experts), name='moe', out_shape=...]
where the time goes in v4:
time: 140 us; the launch traced here: 139 us
  Pallas kernels  139 us (99%)
    pallas_call x1, Pallas kernels, shards(): pl.pallas_call(functools.partial(kernel, experts), name='moe', out_shape=...  136 us

profile of v4, /device:TPU:1, one launch (start us, length us, event | category | flops | bytes accessed | tf_op | source)
XLA Modules:
  0.0 139.4 jit_solution(3782646052237778611)
XLA Ops:
  0.6 136.1 %moe.1 = (bf16[128,1536]{1,0:T(8,128)(2,1)}, bf16[128,1536]{1,0:T(8,128)(2,1)}, f32[128,1536]{1,0:T(8,128)}, f32[128,1536]{1,0:T(8,128)}, f32[2,128]{1,0:T(2,128)}) custom-call(s32[2,128]{1,0:T(2,128)} %bitcast.9, f32[2,128]{1,0:T(2,128)} %bitcast.10, bf16[128,1536]{1,0:T(8,128)(2,1)} %tokens.1, bf16[128,1536]{1,0:T(8,128)(2,1)} %grad_y.1, ...), custom_call_target="tpu_custom_call" | custom-call | tf_op jit(solution)/shard_map/moe/pallas_call | solution.py:516
  136.8 2.6 %place.1 = (f32[128,1536]{1,0:T(8,128)}, f32[128,1536]{1,0:T(8,128)}, bf16[128,1536]{1,0:T(8,128)(2,1)}, bf16[128,1536]{1,0:T(8,128)(2,1)}, f32[2,128]{1,0:T(2,128)}) custom-call(f32[128,1536]{1,0:T(8,128)} %get-tuple-element.15.refs_0_, f32[128,1536]{1,0:T(8,128)} %get-tuple-element.16.refs_1_, bf16[128,1536]{1,0:T(8,128)(2,1)} %get-tuple-element.17.refs_2_, ...), custom_call_target="tpu_custom_call" | custom-call | tf_op jit(solution)/shard_map/place/pallas_call | solution.py:565
